TPU v7x, 32 devices: a whole 2x2x4 slice. The times are simulated.
32 devices in a mesh: row: 4 (over x, core), col: 8 (over z, y).
Axes of the slice: x: 2, y: 2, z: 4, core: 2. Of those that a mesh axis runs over, the one named last changes fastest.
Arguments:
- features: bfloat16 [8192, 256], P(('col', 'row')), may hold values from -6 to 6
- weight: bfloat16 [256, 256], replicated, may hold values from -0.375 to 0.375
- grad_out: bfloat16 [8192, 256], P(('row', 'col')), may hold values from -6 to 6
- adj_values: bfloat16 [384, 1024, 128], P('row', 'col'), may hold values from -0.15625 to 0.15625
- block_pos: int32 [4, 768], P('row', 'col'), may hold values from 0 to 127, as said below
- block_count: int32 [4, 8], P('row', 'col'), may hold values from 24 to 96, as said below
Outputs:
- activation: bfloat16 [8192, 256], P(('row', 'col'))
- grad_input: bfloat16 [8192, 256], P(('col', 'row'))
- grad_weight: float32 [256, 256], replicated
Inputs may be any that keep to these rules, and one draw needn't show every extreme that they name: `block_pos`: within one tile the block positions of all 96 slots are distinct values below 128. `block_count`: some tile has exactly 96 live slots and some tile exactly 24.
All inputs are finite; a program needn't handle non-finite values.
Results may differ from a plain program's by a relative error of at most 0.018.
Values may be sent and summed in bfloat16 or wider, within the bound.
A program may use at most 128 MiB of HBM per device.

v0:
```python
import jax
import jax.numpy as jnp
from jax import lax
from jax.sharding import PartitionSpec as P


def tile_forward(values, positions, live_count, panel, row_blocks, col_blocks):
    slots = values.shape[0]
    block_size = values.shape[1]
    width = panel.shape[1]
    groups = 6
    per_group = slots // groups
    brow = positions // col_blocks
    bcol = positions % col_blocks
    live = (jnp.arange(slots, dtype=jnp.int32) < live_count).astype(jnp.float32)
    blocks = panel.reshape(col_blocks, block_size, width)

    def step(totals, items):
        vals, rows_idx, cols_idx, alive = items
        picked = blocks[cols_idx]
        prod = jnp.einsum("kij,kjf->kif", vals, picked, preferred_element_type=jnp.float32)
        onehot = (rows_idx[None, :] == jnp.arange(row_blocks, dtype=jnp.int32)[:, None]).astype(
            jnp.float32
        ) * alive[None, :]
        return (totals + jnp.einsum("bk,kif->bif", onehot, prod), None)

    items = (
        values.reshape(groups, per_group, block_size, block_size),
        brow.reshape(groups, per_group),
        bcol.reshape(groups, per_group),
        live.reshape(groups, per_group),
    )
    start = jnp.zeros((row_blocks, block_size, width), jnp.float32)
    totals, unused = lax.scan(step, start, items)
    return totals.reshape(row_blocks * block_size, width)


def tile_backward(values, positions, live_count, grads, row_blocks, col_blocks):
    slots = values.shape[0]
    block_size = values.shape[1]
    width = grads.shape[1]
    groups = 6
    per_group = slots // groups
    brow = positions // col_blocks
    bcol = positions % col_blocks
    live = (jnp.arange(slots, dtype=jnp.int32) < live_count).astype(jnp.float32)
    blocks = grads.reshape(row_blocks, block_size, width)

    def step(totals, items):
        vals, rows_idx, cols_idx, alive = items
        picked = blocks[rows_idx]
        prod = jnp.einsum("kij,kif->kjf", vals, picked, preferred_element_type=jnp.float32)
        onehot = (cols_idx[None, :] == jnp.arange(col_blocks, dtype=jnp.int32)[:, None]).astype(
            jnp.float32
        ) * alive[None, :]
        return (totals + jnp.einsum("bk,kjf->bjf", onehot, prod), None)

    items = (
        values.reshape(groups, per_group, block_size, block_size),
        brow.reshape(groups, per_group),
        bcol.reshape(groups, per_group),
        live.reshape(groups, per_group),
    )
    start = jnp.zeros((col_blocks, block_size, width), jnp.float32)
    totals, unused = lax.scan(step, start, items)
    return totals.reshape(col_blocks * block_size, width)


def body(features, weight, grad_out, adj_values, block_pos, block_count):
    block_size = adj_values.shape[2]
    rows_tile = grad_out.shape[0] * lax.axis_size("col")
    row_blocks = rows_tile // block_size
    projected = jnp.dot(features, weight, preferred_element_type=jnp.float32).astype(jnp.bfloat16)
    panel = lax.all_gather(projected, "row", axis=0, tiled=True)
    col_blocks = panel.shape[0] // block_size
    positions = block_pos[0]
    live_count = block_count[0, 0]
    partial_value = tile_forward(adj_values, positions, live_count, panel, row_blocks, col_blocks)
    hidden = lax.psum_scatter(
        partial_value.astype(jnp.bfloat16), "col", scatter_dimension=0, tiled=True
    ).astype(jnp.float32)
    sigma = jax.nn.sigmoid(hidden)
    activation = (hidden * sigma).astype(jnp.bfloat16)
    grad_hidden = (grad_out.astype(jnp.float32) * sigma * (1.0 + hidden * (1.0 - sigma))).astype(
        jnp.bfloat16
    )
    grad_panel = lax.all_gather(grad_hidden, "col", axis=0, tiled=True)
    partial_back = tile_backward(
        adj_values, positions, live_count, grad_panel, row_blocks, col_blocks
    )
    grad_xw = lax.psum_scatter(
        partial_back.astype(jnp.bfloat16), "row", scatter_dimension=0, tiled=True
    )
    local_weight = lax.dot_general(
        features, grad_xw, (((0,), (0,)), ((), ())), preferred_element_type=jnp.float32
    )
    grad_weight = lax.psum(local_weight, ("row", "col"))
    grad_input = lax.dot_general(
        grad_xw, weight, (((1,), (1,)), ((), ())), preferred_element_type=jnp.float32
    ).astype(jnp.bfloat16)
    return (activation, grad_input, grad_weight)


def solution(mesh):
    placed = (
        P(("col", "row"), None),
        P(),
        P(("row", "col"), None),
        P("row", "col", None),
        P("row", "col"),
        P("row", "col"),
    )
    return jax.shard_map(
        body,
        mesh=mesh,
        in_specs=placed,
        out_specs=(P(("row", "col"), None), P(("col", "row"), None), P()),
        check_vma=False,
    )
```

profile of v0, /device:TPU:0, one launch (start us, length us, event | category | flops | bytes accessed | tf_op | source)
XLA Modules:
  0.0 351.3 jit_solution(11104023459522061868)
XLA Ops:
  7.2 0.0 copy-start
  7.2 0.0 reduce-scatter.3.cloned.1.call-start
  7.2 0.5 broadcast.122
  7.7 1.3 reduce.3
  9.1 0.1 squeeze.25
  9.8 1.1 convolution_convert_fusion.1
  10.9 8.6 %all_gather.6 = bf16[1024,256]{1,0:T(8,128)(2,1)S(1)} all-gather(bf16[256,256]{1,0:T(8,128)(2,1)S(1)} %convolution_convert_fusion.1), channel_id=1, replica_groups=mesh['row'=4,'col'=8] {'row'}, dimensions={0}, use_global_device_ids=true | all-gather | bytes 655360 | tf_op jit(solution)/shard_map/all_gather | solution.py:74
  19.6 33.6 %while.22 = (s32[]{:T(128)}, f32[16,128,256]{2,0,1:T(8,128)}, s32[6,16]{1,0:T(8,128)S(1)}, bf16[6,16]{1,0:T(8,128)(2,1)S(1)}, bf16[6,16,128,128]{3,2,1,0:T(8,128...) while((s32[]{:T(128)}, f32[16,128,256]{2,0,1:T(8,128)}, ...), condition=%wide.region_1.2_spmd.clone, body=%wide.region_0.1_spmd.clone.sunk | while | flops 152045104 | bytes 9966739 | solution.py:34
  19.6 0.6 gather_fusion
  20.2 1.5 fusion.77
  21.7 2.1 select_add_fusion.2
  23.9 0.6 gather_fusion
  24.5 1.5 fusion.77
  26.0 3.7 %select_add_fusion.2 = f32[16,128,256]{2,0,1:T(8,128)} fusion(f32[16,128,256]{2,0,1:T(8,128)} %get-tuple-element.261, bf16[16,128,256]{2,1,0:T(8,128)(2,1)S(1)} %fusion.77, pred[]{:T(512)S(6)} %compare.11, bf16[16]{0:T(256)(128)(2,1)S(1)} %fusion.78, s32[16]{0:T(128)S(1)} %fusion.79), kind=kOutput, calls=%fused_computation.4.clone.1 | convolution fusion | flops 17826304 | bytes 5242977 | tf_op jit(solution)/shard_map/while/body/eval_jaxpr/bk,kif->bif/dot_general | solution.py:25
  29.7 0.6 gather_fusion
  30.4 1.5 fusion.77
  31.9 3.7 %select_add_fusion.2 = f32[16,128,256]{2,0,1:T(8,128)} fusion(f32[16,128,256]{2,0,1:T(8,128)} %get-tuple-element.261, bf16[16,128,256]{2,1,0:T(8,128)(2,1)S(1)} %fusion.77, pred[]{:T(512)S(6)} %compare.11, bf16[16]{0:T(256)(128)(2,1)S(1)} %fusion.78, s32[16]{0:T(128)S(1)} %fusion.79), kind=kOutput, calls=%fused_computation.4.clone.1 | convolution fusion | flops 17826304 | bytes 5242977 | tf_op jit(solution)/shard_map/while/body/eval_jaxpr/bk,kif->bif/dot_general | solution.py:25
  35.6 0.6 gather_fusion
  36.2 1.5 fusion.77
  37.7 3.7 %select_add_fusion.2 = f32[16,128,256]{2,0,1:T(8,128)} fusion(f32[16,128,256]{2,0,1:T(8,128)} %get-tuple-element.261, bf16[16,128,256]{2,1,0:T(8,128)(2,1)S(1)} %fusion.77, pred[]{:T(512)S(6)} %compare.11, bf16[16]{0:T(256)(128)(2,1)S(1)} %fusion.78, s32[16]{0:T(128)S(1)} %fusion.79), kind=kOutput, calls=%fused_computation.4.clone.1 | convolution fusion | flops 17826304 | bytes 5242977 | tf_op jit(solution)/shard_map/while/body/eval_jaxpr/bk,kif->bif/dot_general | solution.py:25
  41.5 0.6 gather_fusion
  42.1 1.5 fusion.77
  43.6 3.7 %select_add_fusion.2 = f32[16,128,256]{2,0,1:T(8,128)} fusion(f32[16,128,256]{2,0,1:T(8,128)} %get-tuple-element.261, bf16[16,128,256]{2,1,0:T(8,128)(2,1)S(1)} %fusion.77, pred[]{:T(512)S(6)} %compare.11, bf16[16]{0:T(256)(128)(2,1)S(1)} %fusion.78, s32[16]{0:T(128)S(1)} %fusion.79), kind=kOutput, calls=%fused_computation.4.clone.1 | convolution fusion | flops 17826304 | bytes 5242977 | tf_op jit(solution)/shard_map/while/body/eval_jaxpr/bk,kif->bif/dot_general | solution.py:25
  47.4 0.6 gather_fusion
  48.0 1.5 fusion.77
  49.5 3.7 %select_add_fusion.2 = f32[16,128,256]{2,0,1:T(8,128)} fusion(f32[16,128,256]{2,0,1:T(8,128)} %get-tuple-element.261, bf16[16,128,256]{2,1,0:T(8,128)(2,1)S(1)} %fusion.77, pred[]{:T(512)S(6)} %compare.11, bf16[16]{0:T(256)(128)(2,1)S(1)} %fusion.78, s32[16]{0:T(128)S(1)} %fusion.79), kind=kOutput, calls=%fused_computation.4.clone.1 | convolution fusion | flops 17826304 | bytes 5242977 | tf_op jit(solution)/shard_map/while/body/eval_jaxpr/bk,kif->bif/dot_general | solution.py:25
  53.2 1.7 convert_element_type.39
  54.9 0.0 copy-start.2
  55.0 1.3 copy.11
  56.3 0.0 reduce-scatter.3.cloned.1.call-update
  56.3 0.0 all-gather.2.cloned.1.call-start
  56.4 65.1 %reduce-scatter.3.cloned.1.call-done = bf16[256,256]{1,0:T(8,128)(2,1)} async-done(((bf16[2048,256]{1,0:T(8,128)(2,1)}), bf16[256,256]{1,0:T(8,128)(2,1)}) %reduce-scatter.3.cloned.1.call-update) | async-done | bytes 131088 | tf_op jit(solution)/shard_map/reduce_scatter | solution.py:79
  121.5 1.7 fusion.43
  123.2 0.0 all-gather.2.cloned.1.call-update
  123.2 0.0 reduce-scatter.5.cloned.1.call-start
  123.3 40.2 %all-gather.2.cloned.1.call-done = bf16[2048,256]{1,0:T(8,128)(2,1)} async-done(((bf16[256,256]{1,0:T(8,128)(2,1)}), bf16[2048,256]{1,0:T(8,128)(2,1)}) %all-gather.2.cloned.1.call-update) | async-done | bytes 1048592 | tf_op jit(solution)/shard_map/all_gather | solution.py:87
  163.5 25.3 %while.23 = (s32[]{:T(128)}, f32[8,128,256]{2,0,1:T(8,128)S(1)}, s32[6,16]{1,0:T(8,128)S(1)}, bf16[6,16]{1,0:T(8,128)(2,1)S(1)}, bf16[6,16,128,128]{3,2,1,0:T(8,...) while((s32[]{:T(128)}, f32[8,128,256]{2,0,1:T(8,128)S(1)}, ...), condition=%wide.region_4.5_spmd.clone, body=%wide.region_3.4_spmd.clone.sunk | while | flops 143131952 | bytes 7869587 | solution.py:65
  163.5 1.8 gather_fusion.1
  165.4 1.5 fusion.85
  166.9 0.8 fusion.88
  167.7 1.8 gather_fusion.1
  169.6 1.5 fusion.85
  171.2 0.8 fusion.88
  172.0 1.8 gather_fusion.1
  173.8 1.5 fusion.85
  175.4 0.8 fusion.88
  176.2 1.8 gather_fusion.1
  178.0 1.5 fusion.85
  179.6 0.8 fusion.88
  180.4 1.8 gather_fusion.1
  182.3 1.5 fusion.85
  183.8 0.8 fusion.88
  184.7 1.8 gather_fusion.1
  186.5 1.5 fusion.85
  188.1 0.8 fusion.88
  188.9 1.1 copy.25
  189.9 0.0 reduce-scatter.5.cloned.1.call-update
  190.0 0.0 all-reduce.2.cloned.1.call-start
  190.0 20.4 %reduce-scatter.5.cloned.1.call-done = bf16[256,256]{1,0:T(8,128)(2,1)} async-done(((bf16[1024,256]{1,0:T(8,128)(2,1)}), bf16[256,256]{1,0:T(8,128)(2,1)}) %reduce-scatter.5.cloned.1.call-update) | async-done | bytes 131088 | tf_op jit(solution)/shard_map/reduce_scatter | solution.py:91
  210.5 1.8 convolution_bitcast_fusion
  212.3 0.0 all-reduce.2.cloned.1.call-update
  212.3 1.8 convolution_convert_fusion
  214.1 128.9 %all-reduce.2.cloned.1.call-done = f32[256,256]{0,1:T(8,128)} async-done(((f32[256,256]{0,1:T(8,128)}), f32[256,256]{0,1:T(8,128)}) %all-reduce.2.cloned.1.call-update) | async-done | bytes 262160 | tf_op jit(solution)/shard_map/psum | solution.py:97
  343.0 1.8 copy.13
  (56 shorter events, 0.5 us)
Async XLA Ops:
  7.2 2.7 copy-start
  7.2 114.3 %reduce-scatter.3.cloned.1.call-start = ((), (), s32[]{:S(2)}) async-start(), calls=%async_computation.2 | async-start | bytes 1179648 | tf_op jit(solution)/shard_map/reduce_scatter | solution.py:79
  54.9 66.5 %copy-start.2 = (bf16[256,256]{1,0:T(8,128)(2,1)S(1)}, bf16[256,256]{1,0:T(8,128)(2,1)}, u32[]{:S(2)}) copy-start(bf16[256,256]{1,0:T(8,128)(2,1)} %param.12) | copy-start | bytes 393220
  56.3 107.2 %all-gather.2.cloned.1.call-start = ((), (), s32[]{:S(2)}) async-start(), calls=%async_computation.3 | async-start | bytes 1179648 | tf_op jit(solution)/shard_map/all_gather | solution.py:87
  123.2 87.3 %reduce-scatter.5.cloned.1.call-start = ((), (), s32[]{:S(2)}) async-start(), calls=%async_computation.4 | async-start | bytes 655360 | tf_op jit(solution)/shard_map/reduce_scatter | solution.py:91
  188.8 23.5 %copy-start.1 = (bf16[256,256]{1,0:T(8,128)(2,1)S(1)}, bf16[256,256]{1,0:T(8,128)(2,1)}, u32[]{:S(2)}) copy-start(bf16[256,256]{1,0:T(8,128)(2,1)} %param.11) | copy-start | bytes 393220
  190.0 153.0 %all-reduce.2.cloned.1.call-start = ((), (), s32[]{:S(2)}) async-start(), calls=%async_computation.5 | async-start | bytes 524288 | tf_op jit(solution)/shard_map/psum | solution.py:97
Sparse Core Ops, SparseCore 0:
  56.4 64.9 reduce-scatter.2
  124.2 39.3 all-gather.1
  190.1 20.3 reduce-scatter.4
  216.4 126.5 all-reduce.1
where the time goes:
time: 353 us; the launch traced here: 351 us
  waiting for transfers between devices  255 us (72%)
  matrix products  47.9 us (14%)
  local copies, waits for them, and re-layouts  19.8 us (6%)
  between operations  14.5 us (4%)
  blocking collectives  8.65 us (2%)
  other arithmetic  4.97 us (1%)
    psum x1, waiting for transfers between devices, body(): grad_weight = lax.psum(local_weight, ('row', 'col'))  129 us
    reduce_scatter x1, waiting for transfers between devices, body(): lax.psum_scatter(partial_value.astype(jnp.bfloat16), 'col', scatter_dimen...  65.1 us
    all_gather x1, waiting for transfers between devices, body(): grad_panel = lax.all_gather(grad_hidden, 'col', axis=0, tiled=True)  40.2 us
    dot_general x6, matrix products, step(): return (totals + jnp.einsum('bk,kif->bif', onehot, prod), None)  20.7 us
    reduce_scatter x1, waiting for transfers between devices, body(): lax.psum_scatter(partial_back.astype(jnp.bfloat16), 'row', scatter_dimens...  20.4 us
    gather x6, local copies, waits for them, and re-layouts, step(): picked = blocks[rows_idx]  11 us
    dot_general x6, matrix products, step(): jnp.einsum('kij,kif->kjf', vals, picked, preferred_element_type=jnp.float32)  9.18 us
    dot_general x6, matrix products, step(): jnp.einsum('kij,kjf->kif', vals, picked, preferred_element_type=jnp.float32)  8.8 us
  transfers between devices with their start and end apart: 4, of which 4 were waited for; matrix products, arithmetic and copies ran while one was open for 1% of the time, Pallas kernels for 0%

commit v1 on v0

--- a/solution.py
+++ b/solution.py
@@ -94,7 +94,7 @@
     local_weight = lax.dot_general(
         features, grad_xw, (((0,), (0,)), ((), ())), preferred_element_type=jnp.float32
     )
-    grad_weight = lax.psum(local_weight, ("row", "col"))
+    grad_weight = jnp.sum(lax.all_gather(local_weight, ("row", "col")), axis=0)
     grad_input = lax.dot_general(
         grad_xw, weight, (((1,), (1,)), ((), ())), preferred_element_type=jnp.float32
     ).astype(jnp.bfloat16)

time: 353 us -> 305 us (0.86)
  waiting for transfers between devices: 255 us -> 205 us
  local copies, waits for them, and re-layouts: 19.8 us -> 36.5 us
  matrix products: 47.9 us -> 32.2 us
    psum x1 -> x0, waiting for transfers between devices: 129 us -> none  [body(): grad_weight = lax.psum(local_weight, ('row', 'col'))]
    all_gather x0 -> x1, waiting for transfers between devices: none -> 83.7 us  [body(): grad_weight = jnp.sum(lax.all_gather(local_weight, ('row', 'col')), axis=0)]
    dot_general x6, matrix products: 20.7 us -> 5.35 us  [step(): return (totals + jnp.einsum('bk,kif->bif', onehot, prod), None)]
    unnamed x8 -> x10, local copies, waits for them, and re-layouts: 2.32 us -> 12.8 us
    gather x6, local copies, waits for them, and re-layouts: 3.68 us -> 9.93 us  [step(): picked = blocks[cols_idx]]
    all_gather x1, waiting for transfers between devices: 40.2 us -> 35.6 us  [body(): grad_panel = lax.all_gather(grad_hidden, 'col', axis=0, tiled=True)]
  transfers between devices with their start and end apart: 4 -> 4, of which waited for: 4 -> 4; matrix products, arithmetic and copies ran while one was open for 1% -> 2% of each run, Pallas kernels for 0% -> 0%
where the time goes in v1:
time: 305 us; the launch traced here: 304 us
  waiting for transfers between devices  205 us (67%)
  local copies, waits for them, and re-layouts  36.5 us (12%)
  matrix products  32.2 us (11%)
  between operations  14.5 us (5%)
  blocking collectives  9.1 us (3%)
  other arithmetic  5.3 us (2%)
    all_gather x1, waiting for transfers between devices, body(): grad_weight = jnp.sum(lax.all_gather(local_weight, ('row', 'col')), axis=0)  83.7 us
    reduce_scatter x1, waiting for transfers between devices, body(): lax.psum_scatter(partial_value.astype(jnp.bfloat16), 'col', scatter_dimen...  65.2 us
    all_gather x1, waiting for transfers between devices, body(): grad_panel = lax.all_gather(grad_hidden, 'col', axis=0, tiled=True)  35.6 us
    reduce_scatter x1, waiting for transfers between devices, body(): lax.psum_scatter(partial_back.astype(jnp.bfloat16), 'row', scatter_dimens...  20.4 us
    unnamed x10, local copies, waits for them, and re-layouts  12.8 us
    gather x6, local copies, waits for them, and re-layouts, step(): picked = blocks[rows_idx]  11 us
    gather x6, local copies, waits for them, and re-layouts, step(): picked = blocks[cols_idx]  9.93 us
    all_gather x1, blocking collectives, body(): panel = lax.all_gather(projected, 'row', axis=0, tiled=True)  9.1 us
  transfers between devices with their start and end apart: 4, of which 4 were waited for; matrix products, arithmetic and copies ran while one was open for 2% of the time, Pallas kernels for 0%

profile of v1, /device:TPU:0, one launch (start us, length us, event | category | flops | bytes accessed | tf_op | source)
XLA Modules:
  0.0 303.6 jit_solution(11827327652055357949)
XLA Ops:
  7.2 0.0 reduce-scatter.3.cloned.1.call-start
  7.9 0.5 broadcast.122
  8.4 1.3 reduce.3
  9.8 0.1 squeeze.25
  9.9 1.1 convolution_convert_fusion.1
  11.0 9.1 %all_gather.12 = bf16[1024,256]{1,0:T(8,128)(2,1)} all-gather(bf16[256,256]{1,0:T(8,128)(2,1)S(1)} %convolution_convert_fusion.1), channel_id=1, replica_groups=mesh['row'=4,'col'=8] {'row'}, dimensions={0}, use_global_device_ids=true | all-gather | bytes 655360 | tf_op jit(solution)/shard_map/all_gather | solution.py:74
  20.1 24.7 %while.22 = (s32[]{:T(128)}, f32[16,128,256]{2,0,1:T(8,128)S(1)}, s32[6,16]{1,0:T(8,128)S(1)}, bf16[6,16]{1,0:T(8,128)(2,1)S(1)}, bf16[6,16,128,128]{3,2,1,0:T(8...) while((s32[]{:T(128)}, f32[16,128,256]{2,0,1:T(8,128)S(1)}, ...), condition=%wide.region_1.2_spmd.clone, body=%wide.region_0.1_spmd.clone.sunk | while | flops 152045104 | bytes 9966239 | solution.py:34
  20.1 1.7 gather_fusion
  21.8 1.5 fusion.77
  23.2 0.9 select_add_fusion.2
  24.2 1.7 gather_fusion
  25.9 1.5 fusion.77
  27.3 0.9 select_add_fusion.2
  28.3 1.7 gather_fusion
  30.0 1.5 fusion.77
  31.5 0.9 select_add_fusion.2
  32.4 1.7 gather_fusion
  34.1 1.5 fusion.77
  35.6 0.9 select_add_fusion.2
  36.6 1.7 gather_fusion
  38.2 1.5 fusion.77
  39.7 0.9 select_add_fusion.2
  40.7 1.7 gather_fusion
  42.3 1.5 fusion.77
  43.8 0.9 select_add_fusion.2
  44.7 0.1 convert_element_type.39
  44.9 1.3 copy.16
  46.2 0.0 reduce-scatter.3.cloned.1.call-update
  46.2 0.0 all-gather.4.cloned.1.call-start
  46.3 65.2 %reduce-scatter.3.cloned.1.call-done = bf16[256,256]{1,0:T(8,128)(2,1)} async-done(((bf16[2048,256]{1,0:T(8,128)(2,1)}), bf16[256,256]{1,0:T(8,128)(2,1)}) %reduce-scatter.3.cloned.1.call-update) | async-done | bytes 131088 | tf_op jit(solution)/shard_map/reduce_scatter | solution.py:79
  111.5 1.7 fusion.43
  113.2 0.0 all-gather.4.cloned.1.call-update
  113.2 0.0 reduce-scatter.5.cloned.1.call-start
  113.3 4.6 %copy.14 = bf16[96,128,128]{1,2,0:T(8,128)(2,1)} copy(bf16[96,128,128]{2,1,0:T(8,128)(2,1)} %bitcast.90) | data formatting | bytes 6291456 | tf_op args[3]
  117.9 35.6 %all-gather.4.cloned.1.call-done = bf16[2048,256]{1,0:T(8,128)(2,1)} async-done(((bf16[256,256]{1,0:T(8,128)(2,1)}), bf16[2048,256]{1,0:T(8,128)(2,1)}) %all-gather.4.cloned.1.call-update) | async-done | bytes 1048592 | tf_op jit(solution)/shard_map/all_gather | solution.py:87
  153.5 24.9 %while.23 = (s32[]{:T(128)}, f32[8,128,256]{2,0,1:T(8,128)S(1)}, s32[6,16]{1,0:T(8,128)S(1)}, bf16[6,16]{1,0:T(8,128)(2,1)S(1)}, bf16[6,16,128,128]{2,3,1,0:T(8,...) while((s32[]{:T(128)}, f32[8,128,256]{2,0,1:T(8,128)S(1)}, ...), condition=%wide.region_4.5_spmd.clone, body=%wide.region_3.4_spmd.clone.sunk | while | flops 143131952 | bytes 7869087 | solution.py:65
  153.5 1.8 gather_fusion.1
  155.4 1.5 fusion.85
  156.8 0.8 fusion.88
  157.7 1.8 gather_fusion.1
  159.5 1.5 fusion.85
  161.0 0.8 fusion.88
  161.9 1.8 gather_fusion.1
  163.7 1.5 fusion.85
  165.2 0.8 fusion.88
  166.0 1.8 gather_fusion.1
  167.9 1.5 fusion.85
  169.3 0.8 fusion.88
  170.2 1.8 gather_fusion.1
  172.0 1.5 fusion.85
  173.5 0.8 fusion.88
  174.3 1.8 gather_fusion.1
  176.2 1.5 fusion.85
  177.7 0.8 fusion.88
  178.4 1.1 copy.30
  179.5 0.0 reduce-scatter.5.cloned.1.call-update
  179.6 0.0 all-gather.6.cloned.1.call-start
  179.6 20.4 %reduce-scatter.5.cloned.1.call-done = bf16[256,256]{1,0:T(8,128)(2,1)} async-done(((bf16[1024,256]{1,0:T(8,128)(2,1)}), bf16[256,256]{1,0:T(8,128)(2,1)}) %reduce-scatter.5.cloned.1.call-update) | async-done | bytes 131088 | tf_op jit(solution)/shard_map/reduce_scatter | solution.py:91
  200.0 1.8 convolution_bitcast_fusion
  201.9 1.8 convolution_convert_fusion
  203.7 83.7 %all-gather.6.cloned.1.call-done = f32[8192,256]{0,1:T(8,128)} async-done(((f32[256,256]{0,1:T(8,128)}), f32[8192,256]{0,1:T(8,128)}) %all-gather.6.cloned.1.call-update) | async-done | bytes 8388624 | tf_op jit(solution)/shard_map/all_gather | solution.py:97
  287.4 6.8 %copy.20 = f32[32,8,32,256]{3,2,1,0:T(8,128)S(1)} copy(f32[32,8,32,256]{3,1,2,0:T(8,128)} %bitcast.92) | data formatting | bytes 16777216
  294.3 1.9 bitcast_reduce_fusion
  296.2 0.8 copy.18
  (59 shorter events, 0.5 us)
Async XLA Ops:
  7.2 2.7 copy-start
  7.2 104.3 %reduce-scatter.3.cloned.1.call-start = ((), (), s32[]{:S(2)}) async-start(), calls=%async_computation.2 | async-start | bytes 1179648 | tf_op jit(solution)/shard_map/reduce_scatter | solution.py:79
  44.9 66.6 %copy-start.2 = (bf16[256,256]{1,0:T(8,128)(2,1)S(1)}, bf16[256,256]{1,0:T(8,128)(2,1)}, u32[]{:S(2)}) copy-start(bf16[256,256]{1,0:T(8,128)(2,1)} %param.12) | copy-start | bytes 393220
  46.2 107.3 %all-gather.4.cloned.1.call-start = ((), (), s32[]{:S(2)}) async-start(), calls=%async_computation.3 | async-start | bytes 1179648 | tf_op jit(solution)/shard_map/all_gather | solution.py:87
  113.2 86.8 %reduce-scatter.5.cloned.1.call-start = ((), (), s32[]{:S(2)}) async-start(), calls=%async_computation.4 | async-start | bytes 655360 | tf_op jit(solution)/shard_map/reduce_scatter | solution.py:91
  178.4 23.5 %copy-start.1 = (bf16[256,256]{1,0:T(8,128)(2,1)S(1)}, bf16[256,256]{1,0:T(8,128)(2,1)}, u32[]{:S(2)}) copy-start(bf16[256,256]{1,0:T(8,128)(2,1)} %param.11) | copy-start | bytes 393220
  179.6 107.9 %all-gather.6.cloned.1.call-start = ((), (), s32[]{:S(2)}) async-start(), calls=%async_computation.5 | async-start | bytes 8650752 | tf_op jit(solution)/shard_map/all_gather | solution.py:97
Sparse Core Ops, SparseCore 0:
  46.3 65.0 reduce-scatter.2
  114.2 39.2 all-gather.3
  179.7 20.3 reduce-scatter.4
  203.4 84.0 all-gather.5
